TPU v7x, 32 devices: a whole 2x2x4 slice. The times are simulated.
32 devices in a mesh: groups: 2 (over x), fsdp: 8 (over z, y), dp: 2 (over core).
Axes of the slice: x: 2, y: 2, z: 4, core: 2. Of those that a mesh axis runs over, the one named last changes fastest.
Arguments:
- resid: bfloat16 [512, 5120], P(('groups', 'dp'), 'fsdp'), parts along dimension 0, may hold values from -6 to 6
- hidden_act: bfloat16 [512, 6912], P(('groups', 'dp')), parts along dimension 0, may hold values from -11 to 11
- w_down: bfloat16 [6912, 5120], P(None, 'fsdp'), may hold values from -0.078125 to 0.078125
- norm_gain: bfloat16 [5120], P('fsdp'), may hold values from 0.3 to 4, as said below
- head: bfloat16 [5120, 16384], P(None, 'fsdp'), may hold values from -0.25 to 0.25
- data_ids: int32 [512], P(('groups', 'dp')), parts along dimension 0, may hold values from 0 to 16383
- pseudo_ids: int32 [512], P(('groups', 'dp')), parts along dimension 0, may hold values from 0 to 16383
Outputs:
- scores: float32 [512], P(('groups', 'dp')), parts along dimension 0
There are 2 independent parts, one for each index of `groups`. A program takes and returns all parts, laid end to end along the dimension named above; an argument that names none is the same for every part. Nothing has to cross between parts.
Inputs may be any that keep to these rules, and one draw needn't show every extreme that they name: `norm_gain`: positive gains.
All inputs are finite; a program needn't handle non-finite values.
Results may differ from a plain program's by a relative error of at most 0.012.
Values may be sent and summed in bfloat16 or wider, within the bound.
No kernel may reach another device: no remote copies, remote signals or barrier semaphores. Data moves between devices by JAX's collectives and lax.ppermute only.
A program may use at most 192 MiB of HBM per device.

v0:
```python
import jax
import jax.numpy as jnp
from jax import lax
from jax.sharding import PartitionSpec as P

ITERS = 3
cap_value = 30.0
norm_eps = 1e-05
damping = 0.05


def row_total(values):
    return lax.psum(values, "fsdp")


def per_device(resid, hidden_act, w_down, norm_gain, head, data_ids, pseudo_ids):
    tok_rows = hidden_act.shape[0]
    total_rows = tok_rows * lax.axis_size("dp")
    shard_cols = w_down.shape[1]
    width = shard_cols * lax.axis_size("fsdp")
    vocab_cols = head.shape[1]
    vocab_ids = lax.axis_index("fsdp") * vocab_cols + lax.broadcasted_iota(
        jnp.int32, (1, vocab_cols), 1
    )
    gain = norm_gain.astype(jnp.float32)

    def head_logits(normed_shard):
        return jnp.dot(
            lax.all_gather(normed_shard, "fsdp", axis=1, tiled=True),
            head,
            preferred_element_type=jnp.float32,
        )

    def head_project(weighted):
        return (
            lax.psum_scatter(
                lax.dot_general(
                    head, weighted, (((1,), (1,)), ((), ())), preferred_element_type=jnp.float32
                ).astype(jnp.bfloat16),
                "fsdp",
                scatter_dimension=0,
                tiled=True,
            )
            .astype(jnp.float32)
            .T
        )

    z = resid.astype(jnp.float32) + jnp.dot(hidden_act, w_down, preferred_element_type=jnp.float32)
    inv = lax.rsqrt(row_total(jnp.sum(z * z, axis=1, keepdims=True)) / width + norm_eps)
    normed = (z * inv * gain).astype(jnp.bfloat16)
    capped = cap_value * jnp.tanh(head_logits(normed) / cap_value)
    slope = 1.0 - (capped / cap_value) ** 2
    expval = jnp.exp(capped)
    prob = expval / row_total(jnp.sum(expval, axis=1, keepdims=True))

    def norm_back(upstream):
        scaled = gain * head_project((upstream * slope).astype(jnp.bfloat16))
        mixed = row_total(jnp.sum(z * scaled, axis=1, keepdims=True)) / width
        return inv * scaled - z * inv**3 * mixed

    def tangent(full_vector):
        zv = jnp.dot(hidden_act, full_vector, preferred_element_type=jnp.float32)
        inv_t = -(inv**3) * row_total(jnp.sum(z * zv, axis=1, keepdims=True)) / width
        moved = (gain * (zv * inv + z * inv_t)).astype(jnp.bfloat16)
        return slope * head_logits(moved)

    def full_rows(vector):
        return lax.all_gather(vector.astype(jnp.bfloat16), "dp", axis=0, tiled=True)

    def param_sum(dz):
        local = lax.dot_general(
            hidden_act,
            dz.astype(jnp.bfloat16),
            (((0,), (0,)), ((), ())),
            preferred_element_type=jnp.float32,
        )
        return lax.psum_scatter(
            local.astype(jnp.bfloat16), "dp", scatter_dimension=0, tiled=True
        ).astype(jnp.float32)

    def global_dot(values):
        return lax.psum(values, ("fsdp", "dp"))

    pseudo_hot = (pseudo_ids[:, None] == vocab_ids).astype(jnp.float32)
    grad = param_sum(norm_back((prob - pseudo_hot) / total_rows))
    solution = jnp.zeros_like(grad)
    remain = grad
    search = grad
    norm_now = global_dot(jnp.sum(remain * remain))
    for step in range(ITERS):
        change = tangent(full_rows(search))
        inner = row_total(jnp.sum(prob * change, axis=1, keepdims=True))
        image = param_sum(norm_back((prob * change - prob * inner) / total_rows)) + damping * search
        alpha = norm_now / global_dot(jnp.sum(search * image))
        solution = solution + alpha * search
        remain = remain - alpha * image
        if step + 1 < ITERS:
            norm_next = global_dot(jnp.sum(remain * remain))
            search = remain + norm_next / norm_now * search
            norm_now = norm_next
    data_hot = (data_ids[:, None] == vocab_ids).astype(jnp.float32)
    return row_total(jnp.sum((prob - data_hot) * tangent(full_rows(solution)), axis=1))


def solution(mesh):
    placed = (
        P(("groups", "dp"), "fsdp"),
        P(("groups", "dp"), None),
        P(None, "fsdp"),
        P("fsdp"),
        P(None, "fsdp"),
        P(("groups", "dp")),
        P(("groups", "dp")),
    )
    return jax.shard_map(
        per_device, mesh=mesh, in_specs=placed, out_specs=P(("groups", "dp")), check_vma=False
    )
```

profile of v0, /device:TPU:0, one launch (start us, length us, event | category | flops | bytes accessed | tf_op | source)
XLA Modules:
  0.0 1366.7 jit_solution(14872717110527854634)
XLA Ops:
  13.2 23.2 %psum.140 = f32[128,1]{0,1:T(1,128)S(1)} all-reduce(f32[128,1]{0,1:T(1,128)S(1)} %bitcast.129), channel_id=1, replica_groups=mesh['groups'=2,'fsdp'=8,'dp'=2] {'fsdp'}, use_global_device_ids=true, to_apply=%region_1.0 | all-reduce | flops 128 | bytes 1024 | tf_op jit(solution)/shard_map/psum | solution.py:13
  37.2 39.9 %all-gather.10.cloned.1.call-done = bf16[128,5120]{1,0:T(8,128)(2,1)} async-done(((bf16[128,640]{1,0:T(8,128)(2,1)}), bf16[128,5120]{1,0:T(8,128)(2,1)}) %all-gather.10.cloned.1.call-update) | async-done | bytes 1310736 | tf_op jit(solution)/shard_map/all_gather | solution.py:29
  77.1 11.3 fusion.23
  88.4 19.0 %psum.141 = f32[128]{0:T(128)S(1)} all-reduce(f32[128]{0:T(128)S(1)} %get-tuple-element.17), channel_id=1, replica_groups=mesh['groups'=2,'fsdp'=8,'dp'=2] {'fsdp'}, use_global_device_ids=true, to_apply=%region_3.0 | all-reduce | flops 128 | bytes 1024 | tf_op jit(solution)/shard_map/psum | solution.py:13
  107.4 11.5 fusion.11
  120.5 62.6 %reduce-scatter.25.cloned.1.call-done = bf16[640,128]{1,0:T(8,128)(2,1)} async-done(((bf16[5120,128]{1,0:T(8,128)(2,1)}), bf16[640,128]{1,0:T(8,128)(2,1)}) %reduce-scatter.25.cloned.1.call-update) | async-done | bytes 163856
  184.2 19.0 %psum.142 = f32[128,1]{0,1:T(1,128)S(1)} all-reduce(f32[128,1]{0,1:T(1,128)S(1)} %bitcast.130), channel_id=1, replica_groups=mesh['groups'=2,'fsdp'=8,'dp'=2] {'fsdp'}, use_global_device_ids=true, to_apply=%region_6.0 | all-reduce | flops 128 | bytes 1024 | tf_op jit(solution)/shard_map/psum | solution.py:13
  209.3 12.6 copy.22
  222.0 14.1 %reduce-scatter.27.cloned.1.call-done = bf16[3456,640]{1,0:T(8,128)(2,1)} async-done(((bf16[6912,640]{1,0:T(8,128)(2,1)}), bf16[3456,640]{1,0:T(8,128)(2,1)}) %reduce-scatter.27.cloned.1.call-update) | async-done | bytes 4423696
  243.5 22.2 %all-gather.12.cloned.1.call-done = bf16[6912,640]{0,1:T(8,128)(2,1)} async-done(((bf16[3456,640]{0,1:T(8,128)(2,1)}), bf16[6912,640]{0,1:T(8,128)(2,1)}) %all-gather.12.cloned.1.call-update) | async-done | bytes 8847376 | tf_op jit(solution)/shard_map/all_gather | solution.py:68
  272.1 21.6 %psum.144 = f32[128,1]{0,1:T(1,128)S(1)} all-reduce(f32[128,1]{0,1:T(1,128)S(1)} %bitcast.134), channel_id=1, replica_groups=mesh['groups'=2,'fsdp'=8,'dp'=2] {'fsdp'}, use_global_device_ids=true, to_apply=%region_11.0 | all-reduce | flops 128 | bytes 1024 | tf_op jit(solution)/shard_map/psum | solution.py:13
  294.6 39.9 %all-gather.14.cloned.1.call-done = bf16[128,5120]{1,0:T(8,128)(2,1)} async-done(((bf16[128,640]{1,0:T(8,128)(2,1)}), bf16[128,5120]{1,0:T(8,128)(2,1)}) %all-gather.14.cloned.1.call-update) | async-done | bytes 1310736 | tf_op jit(solution)/shard_map/all_gather | solution.py:29
  334.5 11.5 fusion.82
  346.0 19.0 %psum.145 = f32[128]{0:T(128)S(1)} all-reduce(f32[128]{0:T(128)S(1)} %get-tuple-element.21), channel_id=1, replica_groups=mesh['groups'=2,'fsdp'=8,'dp'=2] {'fsdp'}, use_global_device_ids=true, to_apply=%region_13.0 | all-reduce | flops 128 | bytes 1024 | tf_op jit(solution)/shard_map/psum | solution.py:13
  365.0 11.9 fusion.12
  378.4 62.5 %reduce-scatter.29.cloned.1.call-done = bf16[640,128]{1,0:T(8,128)(2,1)} async-done(((bf16[5120,128]{1,0:T(8,128)(2,1)}), bf16[640,128]{1,0:T(8,128)(2,1)}) %reduce-scatter.29.cloned.1.call-update) | async-done | bytes 163856
  442.1 19.2 %psum.146 = f32[128,1]{0,1:T(1,128)S(1)} all-reduce(f32[128,1]{0,1:T(1,128)S(1)} %bitcast.131), channel_id=1, replica_groups=mesh['groups'=2,'fsdp'=8,'dp'=2] {'fsdp'}, use_global_device_ids=true, to_apply=%region_16.0 | all-reduce | flops 128 | bytes 1024 | tf_op jit(solution)/shard_map/psum | solution.py:13
  467.3 12.6 copy.26
  480.3 13.6 reduce-scatter.31.cloned.1.call-done
  506.5 34.5 %all-reduce = (f32[]{:T(128)}, f32[]{:T(128)}) all-reduce(f32[]{:T(128)} %get-tuple-element.6, f32[]{:T(128)} %get-tuple-element.5), channel_id=1, replica_groups=mesh['groups'=2,'fsdp'=8,'dp'=2] {'fsdp','dp'}, use_global_device_ids=true, to_apply=%region_9.0 | all-reduce | flops 2 | bytes 16 | tf_op jit(solution)/shard_map/psum | solution.py:82
  548.7 30.1 %psum.148 = f32[]{:T(128)} all-reduce(f32[]{:T(128)} %multiply_reduce_fusion.3), channel_id=1, replica_groups=mesh['groups'=2,'fsdp'=8,'dp'=2] {'fsdp','dp'}, use_global_device_ids=true, to_apply=%region_21.0 | all-reduce | flops 1 | bytes 8 | tf_op jit(solution)/shard_map/psum | solution.py:82
  588.4 18.3 %all-gather.16.cloned.1.call-done = bf16[6912,640]{0,1:T(8,128)(2,1)} async-done(((bf16[3456,640]{0,1:T(8,128)(2,1)}), bf16[6912,640]{0,1:T(8,128)(2,1)}) %all-gather.16.cloned.1.call-update) | async-done | bytes 8847376 | tf_op jit(solution)/shard_map/all_gather | solution.py:68
  613.1 21.6 %psum.149 = f32[128,1]{0,1:T(1,128)S(1)} all-reduce(f32[128,1]{0,1:T(1,128)S(1)} %bitcast.135), channel_id=1, replica_groups=mesh['groups'=2,'fsdp'=8,'dp'=2] {'fsdp'}, use_global_device_ids=true, to_apply=%region_23.0 | all-reduce | flops 128 | bytes 1024 | tf_op jit(solution)/shard_map/psum | solution.py:13
  635.6 39.9 %all-gather.18.cloned.1.call-done = bf16[128,5120]{1,0:T(8,128)(2,1)} async-done(((bf16[128,640]{1,0:T(8,128)(2,1)}), bf16[128,5120]{1,0:T(8,128)(2,1)}) %all-gather.18.cloned.1.call-update) | async-done | bytes 1310736 | tf_op jit(solution)/shard_map/all_gather | solution.py:29
  675.5 11.6 fusion.83
  687.0 19.1 %psum.150 = f32[128]{0:T(128)S(1)} all-reduce(f32[128]{0:T(128)S(1)} %get-tuple-element.25), channel_id=1, replica_groups=mesh['groups'=2,'fsdp'=8,'dp'=2] {'fsdp'}, use_global_device_ids=true, to_apply=%region_25.0 | all-reduce | flops 128 | bytes 1024 | tf_op jit(solution)/shard_map/psum | solution.py:13
  706.1 11.9 fusion.13
  719.5 62.5 %reduce-scatter.33.cloned.1.call-done = bf16[640,128]{1,0:T(8,128)(2,1)} async-done(((bf16[5120,128]{1,0:T(8,128)(2,1)}), bf16[640,128]{1,0:T(8,128)(2,1)}) %reduce-scatter.33.cloned.1.call-update) | async-done | bytes 163856
  783.3 19.1 %psum.151 = f32[128,1]{0,1:T(1,128)S(1)} all-reduce(f32[128,1]{0,1:T(1,128)S(1)} %bitcast.132), channel_id=1, replica_groups=mesh['groups'=2,'fsdp'=8,'dp'=2] {'fsdp'}, use_global_device_ids=true, to_apply=%region_28.0 | all-reduce | flops 128 | bytes 1024 | tf_op jit(solution)/shard_map/psum | solution.py:13
  808.4 12.6 copy.30
  821.1 14.1 %reduce-scatter.35.cloned.1.call-done = bf16[3456,640]{1,0:T(8,128)(2,1)} async-done(((bf16[6912,640]{1,0:T(8,128)(2,1)}), bf16[3456,640]{1,0:T(8,128)(2,1)}) %reduce-scatter.35.cloned.1.call-update) | async-done | bytes 4423696
  849.7 34.5 %psum.152 = f32[]{:T(128)} all-reduce(f32[]{:T(128)} %multiply_reduce_fusion.2), channel_id=1, replica_groups=mesh['groups'=2,'fsdp'=8,'dp'=2] {'fsdp','dp'}, use_global_device_ids=true, to_apply=%region_31.0 | all-reduce | flops 1 | bytes 8 | tf_op jit(solution)/shard_map/psum | solution.py:82
  893.3 30.3 %psum.153 = f32[]{:T(128)} all-reduce(f32[]{:T(128)} %multiply_reduce_fusion.1), channel_id=1, replica_groups=mesh['groups'=2,'fsdp'=8,'dp'=2] {'fsdp','dp'}, use_global_device_ids=true, to_apply=%region_33.0 | all-reduce | flops 1 | bytes 8 | tf_op jit(solution)/shard_map/psum | solution.py:82
  935.1 18.4 %all-gather.20.cloned.1.call-done = bf16[6912,640]{0,1:T(8,128)(2,1)} async-done(((bf16[3456,640]{0,1:T(8,128)(2,1)}), bf16[6912,640]{0,1:T(8,128)(2,1)}) %all-gather.20.cloned.1.call-update) | async-done | bytes 8847376 | tf_op jit(solution)/shard_map/all_gather | solution.py:68
  959.9 21.6 %psum.154 = f32[128,1]{0,1:T(1,128)S(1)} all-reduce(f32[128,1]{0,1:T(1,128)S(1)} %bitcast.136), channel_id=1, replica_groups=mesh['groups'=2,'fsdp'=8,'dp'=2] {'fsdp'}, use_global_device_ids=true, to_apply=%region_35.0 | all-reduce | flops 128 | bytes 1024 | tf_op jit(solution)/shard_map/psum | solution.py:13
  982.4 39.9 %all-gather.22.cloned.1.call-done = bf16[128,5120]{1,0:T(8,128)(2,1)} async-done(((bf16[128,640]{1,0:T(8,128)(2,1)}), bf16[128,5120]{1,0:T(8,128)(2,1)}) %all-gather.22.cloned.1.call-update) | async-done | bytes 1310736 | tf_op jit(solution)/shard_map/all_gather | solution.py:29
  1022.2 11.5 fusion.84
  1033.8 19.0 %psum.155 = f32[128]{0:T(128)S(1)} all-reduce(f32[128]{0:T(128)S(1)} %get-tuple-element.29), channel_id=1, replica_groups=mesh['groups'=2,'fsdp'=8,'dp'=2] {'fsdp'}, use_global_device_ids=true, to_apply=%region_37.0 | all-reduce | flops 128 | bytes 1024 | tf_op jit(solution)/shard_map/psum | solution.py:13
  1052.7 11.8 fusion.14
  1066.1 62.5 %reduce-scatter.37.cloned.1.call-done = bf16[640,128]{1,0:T(8,128)(2,1)} async-done(((bf16[5120,128]{1,0:T(8,128)(2,1)}), bf16[640,128]{1,0:T(8,128)(2,1)}) %reduce-scatter.37.cloned.1.call-update) | async-done | bytes 163856
  1129.7 19.5 %psum.156 = f32[128,1]{0,1:T(1,128)S(1)} all-reduce(f32[128,1]{0,1:T(1,128)S(1)} %bitcast.133), channel_id=1, replica_groups=mesh['groups'=2,'fsdp'=8,'dp'=2] {'fsdp'}, use_global_device_ids=true, to_apply=%region_40.0 | all-reduce | flops 128 | bytes 1024 | tf_op jit(solution)/shard_map/psum | solution.py:13
  1155.3 12.5 copy.34
  1167.8 14.0 %reduce-scatter.39.cloned.1.call-done = bf16[3456,640]{1,0:T(8,128)(2,1)} async-done(((bf16[6912,640]{1,0:T(8,128)(2,1)}), bf16[3456,640]{1,0:T(8,128)(2,1)}) %reduce-scatter.39.cloned.1.call-update) | async-done | bytes 4423696
  1196.7 34.5 %psum.157 = f32[]{:T(128)} all-reduce(f32[]{:T(128)} %multiply_reduce_fusion), channel_id=1, replica_groups=mesh['groups'=2,'fsdp'=8,'dp'=2] {'fsdp','dp'}, use_global_device_ids=true, to_apply=%region_43.0 | all-reduce | flops 1 | bytes 8 | tf_op jit(solution)/shard_map/psum | solution.py:82
  1242.1 18.3 %all-gather.24.cloned.1.call-done = bf16[6912,640]{0,1:T(8,128)(2,1)} async-done(((bf16[3456,640]{0,1:T(8,128)(2,1)}), bf16[6912,640]{0,1:T(8,128)(2,1)}) %all-gather.24.cloned.1.call-update) | async-done | bytes 8847376 | tf_op jit(solution)/shard_map/all_gather | solution.py:68
  1266.8 21.9 %psum.158 = f32[128,1]{0,1:T(1,128)S(1)} all-reduce(f32[128,1]{0,1:T(1,128)S(1)} %bitcast.137), channel_id=1, replica_groups=mesh['groups'=2,'fsdp'=8,'dp'=2] {'fsdp'}, use_global_device_ids=true, to_apply=%region_45.0 | all-reduce | flops 128 | bytes 1024 | tf_op jit(solution)/shard_map/psum | solution.py:13
  1289.5 39.9 %all-gather.26.cloned.1.call-done = bf16[128,5120]{1,0:T(8,128)(2,1)} async-done(((bf16[128,640]{1,0:T(8,128)(2,1)}), bf16[128,5120]{1,0:T(8,128)(2,1)}) %all-gather.26.cloned.1.call-update) | async-done | bytes 1310736 | tf_op jit(solution)/shard_map/all_gather | solution.py:29
  1340.2 19.5 %psum.159 = f32[128]{0:T(128)} all-reduce(f32[128]{0:T(128)S(1)} %fusion.21), channel_id=1, replica_groups=mesh['groups'=2,'fsdp'=8,'dp'=2] {'fsdp'}, use_global_device_ids=true, to_apply=%region_47.0 | all-reduce | flops 128 | bytes 1024 | tf_op jit(solution)/shard_map/psum | solution.py:13
  (102 shorter events, 174.6 us)
Async XLA Ops:
  6.5 1.5 copy-start
  6.5 70.6 %all-gather.10.cloned.1.call-start = ((), (), s32[]{:S(2)}) async-start(), calls=%async_computation.8 | async-start | bytes 1474560 | tf_op jit(solution)/shard_map/all_gather | solution.py:29
  37.1 145.9 %reduce-scatter.25.cloned.1.call-start = ((), (), s32[]{:S(2)}) async-start(), calls=%async_computation.17 | async-start | bytes 1474560
  37.2 70.2 %copy-start.5 = (s32[2048]{0:T(1024)}, s32[2048]{0:T(1024)S(1)}, u32[]{:S(2)}) copy-start(s32[2048]{0:T(1024)S(1)} %iota_add_fusion) | copy-start | bytes 24580
  37.2 70.2 %copy-start.7 = (s32[128]{0:T(128)S(1)}, s32[128]{0:T(128)}, u32[]{:S(2)}) copy-start(s32[128]{0:T(128)} %param.13) | copy-start | bytes 1540
  120.4 115.6 %reduce-scatter.27.cloned.1.call-start = ((), (), s32[]{:S(2)}) async-start(), calls=%async_computation.18 | async-start | bytes 13271040
  221.9 43.8 %all-gather.12.cloned.1.call-start = ((), (), s32[]{:S(2)}) async-start(), calls=%async_computation.9 | async-start | bytes 13271040 | tf_op jit(solution)/shard_map/all_gather | solution.py:68
  243.2 91.2 %copy-start.1 = (f32[128,2048]{1,0:T(8,128)S(1)}, f32[128,2048]{1,0:T(8,128)}, u32[]{:S(2)}) copy-start(f32[128,2048]{1,0:T(8,128)} %get-tuple-element.18) | copy-start | bytes 3145732
  243.3 91.2 %all-gather.14.cloned.1.call-start = ((), (), s32[]{:S(2)}) async-start(), calls=%async_computation.10 | async-start | bytes 1474560 | tf_op jit(solution)/shard_map/all_gather | solution.py:29
  294.5 146.3 %reduce-scatter.29.cloned.1.call-start = ((), (), s32[]{:S(2)}) async-start(), calls=%async_computation.19 | async-start | bytes 1474560
  378.4 115.5 %reduce-scatter.31.cloned.1.call-start = ((), (), s32[]{:S(2)}) async-start(), calls=%async_computation.20 | async-start | bytes 13271040
  479.9 126.8 %all-gather.16.cloned.1.call-start = ((), (), s32[]{:S(2)}) async-start(), calls=%async_computation.11 | async-start | bytes 13271040 | tf_op jit(solution)/shard_map/all_gather | solution.py:68
  588.3 87.2 %copy-start.2 = (f32[128,2048]{1,0:T(8,128)S(1)}, f32[128,2048]{1,0:T(8,128)}, u32[]{:S(2)}) copy-start(f32[128,2048]{1,0:T(8,128)} %get-tuple-element.18) | copy-start | bytes 3145732
  588.3 87.2 %all-gather.18.cloned.1.call-start = ((), (), s32[]{:S(2)}) async-start(), calls=%async_computation.12 | async-start | bytes 1474560 | tf_op jit(solution)/shard_map/all_gather | solution.py:29
  635.5 146.6 %reduce-scatter.33.cloned.1.call-start = ((), (), s32[]{:S(2)}) async-start(), calls=%async_computation.21 | async-start | bytes 1474560
  719.5 115.6 %reduce-scatter.35.cloned.1.call-start = ((), (), s32[]{:S(2)}) async-start(), calls=%async_computation.22 | async-start | bytes 13271040
  821.0 132.5 %all-gather.20.cloned.1.call-start = ((), (), s32[]{:S(2)}) async-start(), calls=%async_computation.13 | async-start | bytes 13271040 | tf_op jit(solution)/shard_map/all_gather | solution.py:68
  935.1 87.2 %copy-start.3 = (f32[128,2048]{1,0:T(8,128)S(1)}, f32[128,2048]{1,0:T(8,128)}, u32[]{:S(2)}) copy-start(f32[128,2048]{1,0:T(8,128)} %get-tuple-element.18) | copy-start | bytes 3145732
  935.1 87.2 %all-gather.22.cloned.1.call-start = ((), (), s32[]{:S(2)}) async-start(), calls=%async_computation.14 | async-start | bytes 1474560 | tf_op jit(solution)/shard_map/all_gather | solution.py:29
  982.3 146.2 %reduce-scatter.37.cloned.1.call-start = ((), (), s32[]{:S(2)}) async-start(), calls=%async_computation.23 | async-start | bytes 1474560
  1066.0 115.9 %reduce-scatter.39.cloned.1.call-start = ((), (), s32[]{:S(2)}) async-start(), calls=%async_computation.24 | async-start | bytes 13271040
  1167.8 92.6 %all-gather.24.cloned.1.call-start = ((), (), s32[]{:S(2)}) async-start(), calls=%async_computation.15 | async-start | bytes 13271040 | tf_op jit(solution)/shard_map/all_gather | solution.py:68
  1242.0 87.5 %copy-start.4 = (f32[128,2048]{1,0:T(8,128)S(1)}, f32[128,2048]{1,0:T(8,128)}, u32[]{:S(2)}) copy-start(f32[128,2048]{1,0:T(8,128)} %get-tuple-element.18) | copy-start | bytes 3145732
  1242.0 87.5 %copy-start.6 = (s32[2048]{0:T(1024)S(1)}, s32[2048]{0:T(1024)}, u32[]{:S(2)}) copy-start(s32[2048]{0:T(1024)} %copy-done.5) | copy-start | bytes 24580
  1242.0 87.5 %copy-start.8 = (s32[128]{0:T(128)S(1)}, s32[128]{0:T(128)}, u32[]{:S(2)}) copy-start(s32[128]{0:T(128)} %param.12) | copy-start | bytes 1540
  1242.0 87.4 %all-gather.26.cloned.1.call-start = ((), (), s32[]{:S(2)}) async-start(), calls=%async_computation.16 | async-start | bytes 1474560 | tf_op jit(solution)/shard_map/all_gather | solution.py:29
Sparse Core Ops, SparseCore 0:
  37.2 39.7 all-gather.9
  120.5 62.4 reduce-scatter.24
  222.0 13.9 reduce-scatter.26
  243.4 22.2 all-gather.11
  294.6 39.7 all-gather.13
  378.5 62.3 reduce-scatter.28
  480.0 13.8 reduce-scatter.30
  588.4 18.2 all-gather.15
  635.6 39.7 all-gather.17
  719.6 62.4 reduce-scatter.32
  821.1 13.9 reduce-scatter.34
  935.2 18.2 all-gather.19
  982.4 39.7 all-gather.21
  1066.1 62.3 reduce-scatter.36
  1167.9 13.9 reduce-scatter.38
  1242.1 18.2 all-gather.23
  1289.6 39.7 all-gather.25
where the time goes:
time: 1380 us; the launch traced here: 1370 us
  waiting for transfers between devices  583 us (42%)
  blocking collectives  446 us (32%)
  matrix products  159 us (12%)
  local copies, waits for them, and re-layouts  89.8 us (7%)
  other arithmetic  68 us (5%)
  between operations  20.3 us (1%)
    unnamed x25, waiting for transfers between devices  306 us
    psum x14, blocking collectives, row_total(): return lax.psum(values, 'fsdp')  282 us
    all_gather x5, waiting for transfers between devices, head_logits(): lax.all_gather(normed_shard, 'fsdp', axis=1, tiled=True)  199 us
    psum x5, blocking collectives, global_dot(): return lax.psum(values, ('fsdp', 'dp'))  164 us
    unnamed x34, local copies, waits for them, and re-layouts  89.8 us
    all_gather x4, waiting for transfers between devices, full_rows(): return lax.all_gather(vector.astype(jnp.bfloat16), 'dp', axis=0, tiled=True)  77.2 us
    dot_general x5, matrix products, head_logits(): jnp.dot(lax.all_gather(normed_shard, 'fsdp', axis=1, tiled=True), head, p...  56.8 us
    dot_general x4, matrix products, head_project(): lax.dot_general(head, weighted, (((1,), (1,)), ((), ())), preferred_eleme...  47 us
  transfers between devices with their start and end apart: 17, of which 17 were waited for; matrix products, arithmetic and copies ran while one was open for 0% of the time, Pallas kernels for 0%

commit v1 on v0

--- a/solution.py
+++ b/solution.py
@@ -1,12 +1,21 @@
+import functools
 import jax
 import jax.numpy as jnp
 from jax import lax
 from jax.sharding import PartitionSpec as P
+from jax.lax import psum
 
 ITERS = 3
 cap_value = 30.0
 norm_eps = 1e-05
 damping = 0.05
+
+
+def obtain_the_task(matrix, device_axis, axis_tag):
+    return psum(psum(matrix, device_axis), axis_tag)
+
+
+finish_slabs_in = functools.partial(obtain_the_task, device_axis="dp", axis_tag="fsdp")
 
 
 def row_total(values):
@@ -79,7 +88,7 @@
         ).astype(jnp.float32)
 
     def global_dot(values):
-        return lax.psum(values, ("fsdp", "dp"))
+        return finish_slabs_in(values)
 
     pseudo_hot = (pseudo_ids[:, None] == vocab_ids).astype(jnp.float32)
     grad = param_sum(norm_back((prob - pseudo_hot) / total_rows))

time: 1380 us -> 1330 us (0.964)
  blocking collectives: 446 us -> 400 us
    psum x5 -> x10, blocking collectives: 164 us -> 118 us  [obtain_the_task(): return psum(psum(matrix, device_axis), axis_tag)]
where the time goes in v1:
time: 1330 us; the launch traced here: 1320 us
  waiting for transfers between devices  585 us (44%)
  blocking collectives  400 us (30%)
  matrix products  159 us (12%)
  local copies, waits for them, and re-layouts  89.8 us (7%)
  other arithmetic  67.9 us (5%)
  between operations  20 us (2%)
    unnamed x25, waiting for transfers between devices  306 us
    psum x14, blocking collectives, row_total(): return lax.psum(values, 'fsdp')  282 us
    all_gather x5, waiting for transfers between devices, head_logits(): lax.all_gather(normed_shard, 'fsdp', axis=1, tiled=True)  199 us
    psum x10, blocking collectives, obtain_the_task(): return psum(psum(matrix, device_axis), axis_tag)  118 us
    unnamed x34, local copies, waits for them, and re-layouts  89.8 us
    all_gather x4, waiting for transfers between devices, full_rows(): return lax.all_gather(vector.astype(jnp.bfloat16), 'dp', axis=0, tiled=True)  79.8 us
    dot_general x5, matrix products, head_logits(): jnp.dot(lax.all_gather(normed_shard, 'fsdp', axis=1, tiled=True), head, p...  56.8 us
    dot_general x4, matrix products, head_project(): lax.dot_general(head, weighted, (((1,), (1,)), ((), ())), preferred_eleme...  47 us
  transfers between devices with their start and end apart: 17, of which 17 were waited for; matrix products, arithmetic and copies ran while one was open for 0% of the time, Pallas kernels for 0%

profile of v1, /device:TPU:0, one launch (start us, length us, event | category | flops | bytes accessed | tf_op | source)
XLA Modules:
  0.0 1323.1 jit_solution(2709484673725657721)
XLA Ops:
  13.2 23.2 %psum.182 = f32[128,1]{0,1:T(1,128)S(1)} all-reduce(f32[128,1]{0,1:T(1,128)S(1)} %bitcast.129), channel_id=1, replica_groups=mesh['groups'=2,'fsdp'=8,'dp'=2] {'fsdp'}, use_global_device_ids=true, to_apply=%region_1.0 | all-reduce | flops 128 | bytes 1024 | tf_op jit(solution)/shard_map/psum | solution.py:22
  37.2 39.9 %all-gather.10.cloned.1.call-done = bf16[128,5120]{1,0:T(8,128)(2,1)} async-done(((bf16[128,640]{1,0:T(8,128)(2,1)}), bf16[128,5120]{1,0:T(8,128)(2,1)}) %all-gather.10.cloned.1.call-update) | async-done | bytes 1310736 | tf_op jit(solution)/shard_map/all_gather | solution.py:38
  77.1 11.3 fusion.23
  88.4 19.0 %psum.183 = f32[128]{0:T(128)S(1)} all-reduce(f32[128]{0:T(128)S(1)} %get-tuple-element.19), channel_id=1, replica_groups=mesh['groups'=2,'fsdp'=8,'dp'=2] {'fsdp'}, use_global_device_ids=true, to_apply=%region_3.0 | all-reduce | flops 128 | bytes 1024 | tf_op jit(solution)/shard_map/psum | solution.py:22
  107.4 11.5 fusion.11
  120.4 62.4 %reduce-scatter.25.cloned.1.call-done = bf16[640,128]{1,0:T(8,128)(2,1)} async-done(((bf16[5120,128]{1,0:T(8,128)(2,1)}), bf16[640,128]{1,0:T(8,128)(2,1)}) %reduce-scatter.25.cloned.1.call-update) | async-done | bytes 163856
  184.1 19.1 %psum.184 = f32[128,1]{0,1:T(1,128)S(1)} all-reduce(f32[128,1]{0,1:T(1,128)S(1)} %bitcast.130), channel_id=1, replica_groups=mesh['groups'=2,'fsdp'=8,'dp'=2] {'fsdp'}, use_global_device_ids=true, to_apply=%region_6.0 | all-reduce | flops 128 | bytes 1024 | tf_op jit(solution)/shard_map/psum | solution.py:22
  209.2 12.6 copy.22
  221.8 14.1 %reduce-scatter.27.cloned.1.call-done = bf16[3456,640]{1,0:T(8,128)(2,1)} async-done(((bf16[6912,640]{1,0:T(8,128)(2,1)}), bf16[3456,640]{1,0:T(8,128)(2,1)}) %reduce-scatter.27.cloned.1.call-update) | async-done | bytes 4423696
  243.5 22.1 %all-gather.12.cloned.1.call-done = bf16[6912,640]{0,1:T(8,128)(2,1)} async-done(((bf16[3456,640]{0,1:T(8,128)(2,1)}), bf16[6912,640]{0,1:T(8,128)(2,1)}) %all-gather.12.cloned.1.call-update) | async-done | bytes 8847376 | tf_op jit(solution)/shard_map/all_gather | solution.py:77
  271.9 21.6 %psum.187 = f32[128,1]{0,1:T(1,128)S(1)} all-reduce(f32[128,1]{0,1:T(1,128)S(1)} %bitcast.134), channel_id=1, replica_groups=mesh['groups'=2,'fsdp'=8,'dp'=2] {'fsdp'}, use_global_device_ids=true, to_apply=%region_12.0 | all-reduce | flops 128 | bytes 1024 | tf_op jit(solution)/shard_map/psum | solution.py:22
  294.5 39.9 %all-gather.14.cloned.1.call-done = bf16[128,5120]{1,0:T(8,128)(2,1)} async-done(((bf16[128,640]{1,0:T(8,128)(2,1)}), bf16[128,5120]{1,0:T(8,128)(2,1)}) %all-gather.14.cloned.1.call-update) | async-done | bytes 1310736 | tf_op jit(solution)/shard_map/all_gather | solution.py:38
  334.4 11.5 fusion.82
  345.9 19.0 %psum.188 = f32[128]{0:T(128)S(1)} all-reduce(f32[128]{0:T(128)S(1)} %get-tuple-element.23), channel_id=1, replica_groups=mesh['groups'=2,'fsdp'=8,'dp'=2] {'fsdp'}, use_global_device_ids=true, to_apply=%region_14.0 | all-reduce | flops 128 | bytes 1024 | tf_op jit(solution)/shard_map/psum | solution.py:22
  364.9 11.9 fusion.12
  378.3 62.5 %reduce-scatter.29.cloned.1.call-done = bf16[640,128]{1,0:T(8,128)(2,1)} async-done(((bf16[5120,128]{1,0:T(8,128)(2,1)}), bf16[640,128]{1,0:T(8,128)(2,1)}) %reduce-scatter.29.cloned.1.call-update) | async-done | bytes 163856
  441.9 19.2 %psum.189 = f32[128,1]{0,1:T(1,128)S(1)} all-reduce(f32[128,1]{0,1:T(1,128)S(1)} %bitcast.131), channel_id=1, replica_groups=mesh['groups'=2,'fsdp'=8,'dp'=2] {'fsdp'}, use_global_device_ids=true, to_apply=%region_17.0 | all-reduce | flops 128 | bytes 1024 | tf_op jit(solution)/shard_map/psum | solution.py:22
  467.2 12.6 copy.26
  480.3 13.4 %reduce-scatter.31.cloned.1.call-done = bf16[3456,640]{1,0:T(8,128)(2,1)} async-done(((bf16[6912,640]{1,0:T(8,128)(2,1)}), bf16[3456,640]{1,0:T(8,128)(2,1)}) %reduce-scatter.31.cloned.1.call-update) | async-done | bytes 4423696
  509.5 22.4 %all-reduce = (f32[]{:T(128)}, f32[]{:T(128)}) all-reduce(f32[]{:T(128)} %get-tuple-element.9, f32[]{:T(128)} %get-tuple-element.10), channel_id=1, replica_groups=mesh['groups'=2,'fsdp'=8,'dp'=2] {'fsdp'}, use_global_device_ids=true, to_apply=%region_10.0 | all-reduce | flops 2 | bytes 16 | tf_op jit(solution)/shard_map/psum | solution.py:15
  542.6 17.7 %psum.193 = f32[]{:T(128)} all-reduce(f32[]{:T(128)} %psum.192), channel_id=1, replica_groups=mesh['groups'=2,'fsdp'=8,'dp'=2] {'fsdp'}, use_global_device_ids=true, to_apply=%region_24.0 | all-reduce | flops 1 | bytes 8 | tf_op jit(solution)/shard_map/psum | solution.py:15
  569.9 19.8 %all-gather.16.cloned.1.call-done = bf16[6912,640]{0,1:T(8,128)(2,1)} async-done(((bf16[3456,640]{0,1:T(8,128)(2,1)}), bf16[6912,640]{0,1:T(8,128)(2,1)}) %all-gather.16.cloned.1.call-update) | async-done | bytes 8847376 | tf_op jit(solution)/shard_map/all_gather | solution.py:77
  596.1 21.6 %psum.194 = f32[128,1]{0,1:T(1,128)S(1)} all-reduce(f32[128,1]{0,1:T(1,128)S(1)} %bitcast.135), channel_id=1, replica_groups=mesh['groups'=2,'fsdp'=8,'dp'=2] {'fsdp'}, use_global_device_ids=true, to_apply=%region_26.0 | all-reduce | flops 128 | bytes 1024 | tf_op jit(solution)/shard_map/psum | solution.py:22
  618.8 39.7 %all-gather.18.cloned.1.call-done = bf16[128,5120]{1,0:T(8,128)(2,1)} async-done(((bf16[128,640]{1,0:T(8,128)(2,1)}), bf16[128,5120]{1,0:T(8,128)(2,1)}) %all-gather.18.cloned.1.call-update) | async-done | bytes 1310736 | tf_op jit(solution)/shard_map/all_gather | solution.py:38
  658.5 11.6 fusion.83
  670.0 19.0 %psum.195 = f32[128]{0:T(128)S(1)} all-reduce(f32[128]{0:T(128)S(1)} %get-tuple-element.27), channel_id=1, replica_groups=mesh['groups'=2,'fsdp'=8,'dp'=2] {'fsdp'}, use_global_device_ids=true, to_apply=%region_28.0 | all-reduce | flops 128 | bytes 1024 | tf_op jit(solution)/shard_map/psum | solution.py:22
  689.0 11.8 fusion.13
  702.4 62.5 %reduce-scatter.33.cloned.1.call-done = bf16[640,128]{1,0:T(8,128)(2,1)} async-done(((bf16[5120,128]{1,0:T(8,128)(2,1)}), bf16[640,128]{1,0:T(8,128)(2,1)}) %reduce-scatter.33.cloned.1.call-update) | async-done | bytes 163856
  766.0 19.1 %psum.196 = f32[128,1]{0,1:T(1,128)S(1)} all-reduce(f32[128,1]{0,1:T(1,128)S(1)} %bitcast.132), channel_id=1, replica_groups=mesh['groups'=2,'fsdp'=8,'dp'=2] {'fsdp'}, use_global_device_ids=true, to_apply=%region_31.0 | all-reduce | flops 128 | bytes 1024 | tf_op jit(solution)/shard_map/psum | solution.py:22
  791.2 12.6 copy.30
  803.9 14.0 %reduce-scatter.35.cloned.1.call-done = bf16[3456,640]{1,0:T(8,128)(2,1)} async-done(((bf16[6912,640]{1,0:T(8,128)(2,1)}), bf16[3456,640]{1,0:T(8,128)(2,1)}) %reduce-scatter.35.cloned.1.call-update) | async-done | bytes 4423696
  835.6 22.6 %psum.198 = f32[]{:T(128)} all-reduce(f32[]{:T(128)} %psum.197), channel_id=1, replica_groups=mesh['groups'=2,'fsdp'=8,'dp'=2] {'fsdp'}, use_global_device_ids=true, to_apply=%region_35.0 | all-reduce | flops 1 | bytes 8 | tf_op jit(solution)/shard_map/psum | solution.py:15
  870.4 17.8 %psum.200 = f32[]{:T(128)} all-reduce(f32[]{:T(128)} %psum.199), channel_id=1, replica_groups=mesh['groups'=2,'fsdp'=8,'dp'=2] {'fsdp'}, use_global_device_ids=true, to_apply=%region_38.0 | all-reduce | flops 1 | bytes 8 | tf_op jit(solution)/shard_map/psum | solution.py:15
  899.7 19.8 %all-gather.20.cloned.1.call-done = bf16[6912,640]{0,1:T(8,128)(2,1)} async-done(((bf16[3456,640]{0,1:T(8,128)(2,1)}), bf16[6912,640]{0,1:T(8,128)(2,1)}) %all-gather.20.cloned.1.call-update) | async-done | bytes 8847376 | tf_op jit(solution)/shard_map/all_gather | solution.py:77
  925.8 21.6 %psum.201 = f32[128,1]{0,1:T(1,128)S(1)} all-reduce(f32[128,1]{0,1:T(1,128)S(1)} %bitcast.136), channel_id=1, replica_groups=mesh['groups'=2,'fsdp'=8,'dp'=2] {'fsdp'}, use_global_device_ids=true, to_apply=%region_40.0 | all-reduce | flops 128 | bytes 1024 | tf_op jit(solution)/shard_map/psum | solution.py:22
  948.3 39.9 %all-gather.22.cloned.1.call-done = bf16[128,5120]{1,0:T(8,128)(2,1)} async-done(((bf16[128,640]{1,0:T(8,128)(2,1)}), bf16[128,5120]{1,0:T(8,128)(2,1)}) %all-gather.22.cloned.1.call-update) | async-done | bytes 1310736 | tf_op jit(solution)/shard_map/all_gather | solution.py:38
  988.2 11.5 fusion.84
  999.7 19.4 %psum.202 = f32[128]{0:T(128)S(1)} all-reduce(f32[128]{0:T(128)S(1)} %get-tuple-element.31), channel_id=1, replica_groups=mesh['groups'=2,'fsdp'=8,'dp'=2] {'fsdp'}, use_global_device_ids=true, to_apply=%region_42.0 | all-reduce | flops 128 | bytes 1024 | tf_op jit(solution)/shard_map/psum | solution.py:22
  1019.1 11.8 fusion.14
  1032.4 62.4 %reduce-scatter.37.cloned.1.call-done = bf16[640,128]{1,0:T(8,128)(2,1)} async-done(((bf16[5120,128]{1,0:T(8,128)(2,1)}), bf16[640,128]{1,0:T(8,128)(2,1)}) %reduce-scatter.37.cloned.1.call-update) | async-done | bytes 163856
  1096.0 19.3 %psum.203 = f32[128,1]{0,1:T(1,128)S(1)} all-reduce(f32[128,1]{0,1:T(1,128)S(1)} %bitcast.133), channel_id=1, replica_groups=mesh['groups'=2,'fsdp'=8,'dp'=2] {'fsdp'}, use_global_device_ids=true, to_apply=%region_45.0 | all-reduce | flops 128 | bytes 1024 | tf_op jit(solution)/shard_map/psum | solution.py:22
  1121.4 12.5 copy.34
  1133.9 14.0 %reduce-scatter.39.cloned.1.call-done = bf16[3456,640]{1,0:T(8,128)(2,1)} async-done(((bf16[6912,640]{1,0:T(8,128)(2,1)}), bf16[3456,640]{1,0:T(8,128)(2,1)}) %reduce-scatter.39.cloned.1.call-update) | async-done | bytes 4423696
  1165.8 22.3 %psum.205 = f32[]{:T(128)} all-reduce(f32[]{:T(128)} %psum.204), channel_id=1, replica_groups=mesh['groups'=2,'fsdp'=8,'dp'=2] {'fsdp'}, use_global_device_ids=true, to_apply=%region_49.0 | all-reduce | flops 1 | bytes 8 | tf_op jit(solution)/shard_map/psum | solution.py:15
  1199.2 18.2 %all-gather.24.cloned.1.call-done = bf16[6912,640]{0,1:T(8,128)(2,1)} async-done(((bf16[3456,640]{0,1:T(8,128)(2,1)}), bf16[6912,640]{0,1:T(8,128)(2,1)}) %all-gather.24.cloned.1.call-update) | async-done | bytes 8847376 | tf_op jit(solution)/shard_map/all_gather | solution.py:77
  1223.8 21.6 %psum.206 = f32[128,1]{0,1:T(1,128)S(1)} all-reduce(f32[128,1]{0,1:T(1,128)S(1)} %bitcast.137), channel_id=1, replica_groups=mesh['groups'=2,'fsdp'=8,'dp'=2] {'fsdp'}, use_global_device_ids=true, to_apply=%region_51.0 | all-reduce | flops 128 | bytes 1024 | tf_op jit(solution)/shard_map/psum | solution.py:22
  1246.2 40.0 %all-gather.26.cloned.1.call-done = bf16[128,5120]{1,0:T(8,128)(2,1)} async-done(((bf16[128,640]{1,0:T(8,128)(2,1)}), bf16[128,5120]{1,0:T(8,128)(2,1)}) %all-gather.26.cloned.1.call-update) | async-done | bytes 1310736 | tf_op jit(solution)/shard_map/all_gather | solution.py:38
  1296.9 19.5 %psum.207 = f32[128]{0:T(128)} all-reduce(f32[128]{0:T(128)S(1)} %fusion.21), channel_id=1, replica_groups=mesh['groups'=2,'fsdp'=8,'dp'=2] {'fsdp'}, use_global_device_ids=true, to_apply=%region_53.0 | all-reduce | flops 128 | bytes 1024 | tf_op jit(solution)/shard_map/psum | solution.py:22
  (107 shorter events, 190.6 us)
Async XLA Ops:
  6.5 1.5 copy-start
  6.5 70.6 %all-gather.10.cloned.1.call-start = ((), (), s32[]{:S(2)}) async-start(), calls=%async_computation.8 | async-start | bytes 1474560 | tf_op jit(solution)/shard_map/all_gather | solution.py:38
  37.1 145.8 %reduce-scatter.25.cloned.1.call-start = ((), (), s32[]{:S(2)}) async-start(), calls=%async_computation.17 | async-start | bytes 1474560
  37.2 70.2 %copy-start.5 = (s32[2048]{0:T(1024)}, s32[2048]{0:T(1024)S(1)}, u32[]{:S(2)}) copy-start(s32[2048]{0:T(1024)S(1)} %iota_add_fusion) | copy-start | bytes 24580
  37.2 70.2 %copy-start.7 = (s32[128]{0:T(128)S(1)}, s32[128]{0:T(128)}, u32[]{:S(2)}) copy-start(s32[128]{0:T(128)} %param.13) | copy-start | bytes 1540
  120.4 115.5 %reduce-scatter.27.cloned.1.call-start = ((), (), s32[]{:S(2)}) async-start(), calls=%async_computation.18 | async-start | bytes 13271040
  221.8 43.8 %all-gather.12.cloned.1.call-start = ((), (), s32[]{:S(2)}) async-start(), calls=%async_computation.9 | async-start | bytes 13271040 | tf_op jit(solution)/shard_map/all_gather | solution.py:77
  243.1 91.3 %copy-start.1 = (f32[128,2048]{1,0:T(8,128)S(1)}, f32[128,2048]{1,0:T(8,128)}, u32[]{:S(2)}) copy-start(f32[128,2048]{1,0:T(8,128)} %get-tuple-element.20) | copy-start | bytes 3145732
  243.1 91.2 %all-gather.14.cloned.1.call-start = ((), (), s32[]{:S(2)}) async-start(), calls=%async_computation.10 | async-start | bytes 1474560 | tf_op jit(solution)/shard_map/all_gather | solution.py:38
  294.4 146.3 %reduce-scatter.29.cloned.1.call-start = ((), (), s32[]{:S(2)}) async-start(), calls=%async_computation.19 | async-start | bytes 1474560
  378.2 115.5 %reduce-scatter.31.cloned.1.call-start = ((), (), s32[]{:S(2)}) async-start(), calls=%async_computation.20 | async-start | bytes 13271040
  479.8 109.9 %all-gather.16.cloned.1.call-start = ((), (), s32[]{:S(2)}) async-start(), calls=%async_computation.11 | async-start | bytes 13271040 | tf_op jit(solution)/shard_map/all_gather | solution.py:77
  569.9 88.6 %copy-start.2 = (f32[128,2048]{1,0:T(8,128)S(1)}, f32[128,2048]{1,0:T(8,128)}, u32[]{:S(2)}) copy-start(f32[128,2048]{1,0:T(8,128)} %get-tuple-element.20) | copy-start | bytes 3145732
  569.9 88.6 %all-gather.18.cloned.1.call-start = ((), (), s32[]{:S(2)}) async-start(), calls=%async_computation.12 | async-start | bytes 1474560 | tf_op jit(solution)/shard_map/all_gather | solution.py:38
  618.5 146.3 %reduce-scatter.33.cloned.1.call-start = ((), (), s32[]{:S(2)}) async-start(), calls=%async_computation.21 | async-start | bytes 1474560
  702.3 115.6 %reduce-scatter.35.cloned.1.call-start = ((), (), s32[]{:S(2)}) async-start(), calls=%async_computation.22 | async-start | bytes 13271040
  803.8 115.6 %all-gather.20.cloned.1.call-start = ((), (), s32[]{:S(2)}) async-start(), calls=%async_computation.13 | async-start | bytes 13271040 | tf_op jit(solution)/shard_map/all_gather | solution.py:77
  899.6 88.6 %copy-start.3 = (f32[128,2048]{1,0:T(8,128)S(1)}, f32[128,2048]{1,0:T(8,128)}, u32[]{:S(2)}) copy-start(f32[128,2048]{1,0:T(8,128)} %get-tuple-element.20) | copy-start | bytes 3145732
  899.6 88.6 %all-gather.22.cloned.1.call-start = ((), (), s32[]{:S(2)}) async-start(), calls=%async_computation.14 | async-start | bytes 1474560 | tf_op jit(solution)/shard_map/all_gather | solution.py:38
  948.2 146.6 %reduce-scatter.37.cloned.1.call-start = ((), (), s32[]{:S(2)}) async-start(), calls=%async_computation.23 | async-start | bytes 1474560
  1032.3 115.6 %reduce-scatter.39.cloned.1.call-start = ((), (), s32[]{:S(2)}) async-start(), calls=%async_computation.24 | async-start | bytes 13271040
  1133.9 83.5 %all-gather.24.cloned.1.call-start = ((), (), s32[]{:S(2)}) async-start(), calls=%async_computation.15 | async-start | bytes 13271040 | tf_op jit(solution)/shard_map/all_gather | solution.py:77
  1198.9 87.2 %copy-start.4 = (f32[128,2048]{1,0:T(8,128)S(1)}, f32[128,2048]{1,0:T(8,128)}, u32[]{:S(2)}) copy-start(f32[128,2048]{1,0:T(8,128)} %get-tuple-element.20) | copy-start | bytes 3145732
  1199.0 87.2 %copy-start.6 = (s32[2048]{0:T(1024)S(1)}, s32[2048]{0:T(1024)}, u32[]{:S(2)}) copy-start(s32[2048]{0:T(1024)} %copy-done.5) | copy-start | bytes 24580
  1199.0 87.2 %copy-start.8 = (s32[128]{0:T(128)S(1)}, s32[128]{0:T(128)}, u32[]{:S(2)}) copy-start(s32[128]{0:T(128)} %param.12) | copy-start | bytes 1540
  1199.0 87.2 %all-gather.26.cloned.1.call-start = ((), (), s32[]{:S(2)}) async-start(), calls=%async_computation.16 | async-start | bytes 1474560 | tf_op jit(solution)/shard_map/all_gather | solution.py:38
Sparse Core Ops, SparseCore 0:
  37.2 39.8 all-gather.9
  120.5 62.3 reduce-scatter.24
  221.9 13.9 reduce-scatter.26
  243.2 22.2 all-gather.11
  294.5 39.7 all-gather.13
  378.4 62.3 reduce-scatter.28
  479.9 13.8 reduce-scatter.30
  570.0 19.6 all-gather.15
  618.7 39.7 all-gather.17
  702.5 62.3 reduce-scatter.32
  803.9 13.9 reduce-scatter.34
  899.7 19.6 all-gather.19
  948.4 39.7 all-gather.21
  1032.5 62.2 reduce-scatter.36
  1134.0 13.8 reduce-scatter.38
  1199.1 18.2 all-gather.23
  1246.3 39.7 all-gather.25
